TPU v7x, 32 devices: a whole 2x2x4 slice. The times are simulated.
32 devices in a mesh: group: 4 (over y, x), dev: 8 (over z, core).
Axes of the slice: x: 2, y: 2, z: 4, core: 2. Of those that a mesh axis runs over, the one named last changes fastest.
Arguments:
- member_pressure_heads: float32 [192, 128, 768], P('group', 'dev'), may hold values from -4 to 1
- soil_index: int32 [128, 768], P('dev'), may hold values from 0 to 7
- ks_table: float32 [8], replicated, may hold values from 0.05 to 0.5
- alpha_table: float32 [8], replicated, may hold values from 0.5 to 3
- obs_op: float32 [128, 6, 32, 128], P(('dev', 'group')), may hold values from -0.1875 to 0.1875
- obs_mask: int32 [128, 6], P(('dev', 'group')), may hold values from 0 to 1
- obs_values: float32 [128, 6, 32], P(('dev', 'group')), may hold values from -6 to 6
Outputs:
- analysis: float32 [192, 128, 768], P('group', 'dev')
All inputs are finite; a program needn't handle non-finite values.
Results may differ from a plain program's by a relative error of at most 0.0003.
Values sent between devices are 32-bit elements; how exact they have to be, the bound alone decides.
A program may use at most 64 MiB of HBM per device.

v0:
```python
import jax
import jax.numpy as jnp
from jax import lax
from jax.sharding import PartitionSpec as P

MEMBERS = 192
SOIL_TYPES = 8
MODEL_STEPS = 3
NEWTON_STEPS = 12
BLOCKS = 6


step_duration = 0.1
gravity_head = 1.0
highest = lax.Precision.HIGHEST


def padded(cells, sides, width):
    for axis, dim in sides:
        count = lax.axis_size(axis)
        ends = count - 1
        head = lax.slice_in_dim(cells, 0, width, axis=dim)
        tail = lax.slice_in_dim(cells, cells.shape[dim] - width, cells.shape[dim], axis=dim)
        cells = jnp.concatenate(
            [
                lax.ppermute(tail, axis, [(i, (i + 1) % count) for i in range(ends)]),
                cells,
                lax.ppermute(head, axis, [((i + 1) % count, i) for i in range(ends)]),
            ],
            axis=dim,
        )
    return cells


def soil_values(soil_index, ks_table, alpha_table):
    soil_kinds = jnp.arange(SOIL_TYPES, dtype=jnp.int32)
    one_hot = (soil_index[None] == soil_kinds[:, None, None]).astype(jnp.float32)
    hydraulic_conductance = jnp.sum(one_hot * ks_table[:, None, None], axis=0)
    retention_shape = jnp.sum(one_hot * alpha_table[:, None, None], axis=0)
    return (hydraulic_conductance, retention_shape)


def soil_hydraulic_law(heads_now, hydraulic_conductance, retention_shape):
    factor = jnp.exp(retention_shape * jnp.minimum(heads_now, 0.0))
    return (hydraulic_conductance * factor, 0.1 + 0.4 * retention_shape * factor)


def surface_recharge(padded_heads, padded_k):
    middle = padded_heads[:, 1:-1]
    k_middle = padded_k[:, 1:-1]
    across = 0.5 * (k_middle + padded_k[:, 2:]) * (padded_heads[:, 2:] - middle)
    across = across + 0.5 * (k_middle + padded_k[:, :-2]) * (padded_heads[:, :-2] - middle)
    k_face = 0.5 * (k_middle[..., 1:] + k_middle[..., :-1])
    vertical = k_face * (middle[..., 1:] - middle[..., :-1] - gravity_head)
    border = jnp.zeros_like(middle[..., :1])
    return (
        across + jnp.concatenate([vertical, border], -1) - jnp.concatenate([border, vertical], -1)
    )


def newton_weights(gram_matrix, gram_rhs):
    order_m = gram_matrix.shape[0]
    identity_m = jnp.eye(order_m, dtype=jnp.float32)
    norm_total = jnp.sum(jnp.abs(gram_matrix))

    def one_turn(counter, iterate_pair):
        iterate, inverse = iterate_pair
        middle = 0.5 * (
            3.0 * identity_m
            - jnp.dot(inverse, iterate, precision=highest, preferred_element_type=jnp.float32)
        )
        return (
            jnp.dot(iterate, middle, precision=highest, preferred_element_type=jnp.float32),
            jnp.dot(middle, inverse, precision=highest, preferred_element_type=jnp.float32),
        )

    iterate, inverse = lax.fori_loop(
        0, NEWTON_STEPS, one_turn, (gram_matrix / norm_total, identity_m)
    )
    inner_w = jnp.dot(inverse, gram_rhs, precision=highest, preferred_element_type=jnp.float32)
    shift_w = (
        jnp.dot(inverse, inner_w, precision=highest, preferred_element_type=jnp.float32)
        / norm_total
    )
    return jnp.sqrt((order_m - 1.0) / norm_total) * inverse + shift_w[:, None]


def march_forward(heads_now, hydraulic_conductance, retention_shape):
    ext_heads, ext_conduct, ext_shape = (
        padded(heads_now, (("dev", 1),), MODEL_STEPS),
        padded(hydraulic_conductance[None], (("dev", 1),), MODEL_STEPS),
        padded(retention_shape[None], (("dev", 1),), MODEL_STEPS),
    )
    local_rows = heads_now.shape[1]
    first_row = lax.axis_index("dev") * local_rows - MODEL_STEPS
    grid_total = local_rows * lax.axis_size("dev")
    for counter in range(MODEL_STEPS):
        conductivity_field, moisture_capacity = soil_hydraulic_law(
            ext_heads, ext_conduct, ext_shape
        )
        updated = (
            ext_heads[:, 1:-1]
            + step_duration
            * surface_recharge(ext_heads, conductivity_field)
            / moisture_capacity[:, 1:-1]
        )
        row_ids = first_row + counter + 1 + jnp.arange(updated.shape[1], dtype=jnp.int32)
        inside = (row_ids >= 0) & (row_ids < grid_total)
        ext_heads = jnp.where(inside[None, :, None], updated, 0.0)
        ext_conduct = ext_conduct[:, 1:-1]
        ext_shape = ext_shape[:, 1:-1]
    return ext_heads


def body(member_pressure_heads, soil_index, ks_table, alpha_table, obs_op, obs_mask, obs_values):
    hydraulic_conductance, retention_shape = soil_values(soil_index, ks_table, alpha_table)
    predict_heads = march_forward(member_pressure_heads, hydraulic_conductance, retention_shape)
    mask_float = obs_mask.astype(jnp.float32)
    masked_op = obs_op * mask_float[:, :, None, None]
    masked_values = obs_values * mask_float[:, :, None]
    identity_m = jnp.eye(MEMBERS, dtype=jnp.float32)
    collected_heads = lax.all_to_all(
        predict_heads, "group", split_axis=1, concat_axis=0, tiled=True
    )
    server_rows = collected_heads.shape[1]
    ensemble_average = jnp.sum(collected_heads, axis=0) / MEMBERS
    member_anomalies = collected_heads - ensemble_average
    projected = jnp.einsum(
        "rboc,mrbc->rbom",
        masked_op,
        member_anomalies.reshape(MEMBERS, server_rows, BLOCKS, 128),
        precision=highest,
    ).reshape(-1, MEMBERS)
    innovation = (
        masked_values
        - jnp.einsum(
            "rboc,rbc->rbo",
            masked_op,
            ensemble_average.reshape(server_rows, BLOCKS, 128),
            precision=highest,
        )
    ).reshape(-1)
    gram_part = jnp.dot(
        projected.T, projected, precision=highest, preferred_element_type=jnp.float32
    )
    rhs_part = jnp.dot(
        projected.T, innovation, precision=highest, preferred_element_type=jnp.float32
    )
    gram_total, rhs_total = lax.psum((gram_part, rhs_part), ("group", "dev"))
    mixing = newton_weights(gram_total + (MEMBERS - 1.0) * identity_m, rhs_total)
    mixed = jnp.dot(
        mixing.T,
        member_anomalies.reshape(MEMBERS, -1),
        precision=highest,
        preferred_element_type=jnp.float32,
    )
    analysis = mixed.reshape(collected_heads.shape)
    return lax.all_to_all(analysis, "group", split_axis=0, concat_axis=1, tiled=True)


def solution(mesh):
    placed = (
        P("group", "dev", None),
        P("dev", None),
        P(),
        P(),
        P(("dev", "group"), None, None, None),
        P(("dev", "group"), None),
        P(("dev", "group"), None, None),
    )
    return jax.shard_map(
        body, mesh=mesh, in_specs=placed, out_specs=P("group", "dev", None), check_vma=False
    )
```

profile of v0, /device:TPU:0, one launch (start us, length us, event | category | flops | bytes accessed | tf_op | source)
XLA Modules:
  0.0 297.2 jit_solution(1191694890431882914)
XLA Ops:
  8.1 2.4 collective-permute-start.4
  10.5 1.3 collective-permute-start.5
  12.4 5.2 %collective-permute-start.2 = (f32[1,3,768]{2,1,0:T(4,128)}, f32[1,3,768]{2,1,0:T(4,128)S(1)}, u32[]{:S(2)}, u32[]{:S(2)}) collective-permute-start(f32[1,3,768]{2,1,0:T(4,128)} %get-tuple-element.78), channel_id=1, source_target_pairs={{0,1},{1,2},{2,3},{3,4},{4,5},{5,6},{6,7},{8,9},{9,10},{10,11},{11... | collective-permute-start | bytes 27656 | tf_op jit(solution)/shard_map/ppermute | solution.py:26
  17.6 1.3 collective-permute-start.3
  18.9 1.8 fusion.69
  21.6 4.4 %collective-permute-start = (f32[48,3,768]{2,0,1:T(8,128)}, f32[48,3,768]{2,0,1:T(8,128)S(1)}, u32[]{:S(2)}, u32[]{:S(2)}) collective-permute-start(f32[48,3,768]{2,0,1:T(8,128)} %copy.64), channel_id=1, source_target_pairs={{0,1},{1,2},{2,3},{3,4},{4,5},{5,6},{6,7},{8,9},{9,10},{10,11},{11... | collective-permute-start | bytes 1327112 | tf_op jit(solution)/shard_map/ppermute | solution.py:26
  27.3 1.3 collective-permute-start.1
  31.3 1.4 constant_dynamic-update-slice_fusion.1
  33.7 1.6 fusion.8
  35.3 5.0 %broadcast_multiply_fusion.1 = (f32[48,20,768]{2,0,1:T(8,128)S(1)}, f32[48,20,768]{2,0,1:T(8,128)}, f32[48,20,768]{2,0,1:T(8,128)S(1)}) fusion(f32[20,768]{1,0:T(8,128)S(1)} %copy-done.7, f32[20,768]{1,0:T(8,128)S(1)} %get-tuple-element.71, f32[48,22,768]{2,0,1:T(8,128)S(1)} %get-tuple-element.63, f32[20,768]{1,0:T(8,128)S(1)} %copy-done.6, ...), kind=kLoop, calls=%fused_computation.81 | loop fusion | flops 14745600 | bytes 32620820 | tf_op jit(solution)/shard_map/mul | solution.py:45
  40.4 1.4 fusion.23
  42.2 3.2 %broadcast_multiply_fusion.2 = (f32[48,18,768]{2,0,1:T(8,128)S(1)}, f32[48,18,768]{2,0,1:T(8,128)S(1)}, f32[48,18,768]{2,0,1:T(8,128)S(1)}) fusion(f32[18,768]{1,0:T(8,128)S(1)} %slice_bitcast_fusion, f32[18,768]{1,0:T(8,128)S(1)} %get-tuple-element.69, f32[48,20,768]{2,0,1:T(8,128)S(1)} %copy-done.2, f32[18,768]{1,0:T(8,128)S(1)} %copy-done.5, ...), kind=kLoop, calls=%fused_computation.82 | loop fusion | flops 13271040 | bytes 29358738 | tf_op jit(solution)/shard_map/mul | solution.py:45
  46.8 3.7 %fusion.39 = f32[48,16,768]{2,0,1:T(8,128)} fusion(f32[48,18,768]{2,0,1:T(8,128)S(1)} %get-tuple-element.57, f32[48,18,768]{2,0,1:T(8,128)S(1)} %get-tuple-element.58, f32[48,18,768]{2,0,1:T(8,128)S(1)} %get-tuple-element.56, f32[48,16,767]{2,0,1:T(8,128)S(1)} %fusion.41, f32[16,768]{1,0:T(8,128)S(1)} %copy-done.8, pred[16]{0:T(512)(128)(4,1)S(1)} %compare_and_fusion.2), kind=kLoop, calls=%fused_computation.59 | loop fusion | flops 10027008 | bytes 21279760 | tf_op jit(solution)/shard_map/jit(_where)/select_n | solution.py:109
  50.4 3.8 %all-to-all-start = ((f32[48,16,768]{2,0,1:T(8,128)}), f32[48,16,768]{2,0,1:T(8,128)S(1)}, u32[]{:S(2)}, u32[]{:S(2)}) async-start(f32[48,16,768]{2,0,1:T(8,128)} %fusion.39), calls=%async_computation | async-start | bytes 4718592 | tf_op jit(solution)/shard_map/all_to_all | solution.py:122
  54.5 27.8 %all-to-all-done = f32[48,16,768]{2,0,1:T(8,128)S(1)} async-done(((f32[48,16,768]{2,0,1:T(8,128)}), f32[48,16,768]{2,0,1:T(8,128)S(1)}, u32[]{:S(2)}, u32[]{:S(2)}) %all-to-all-start) | async-done | bytes 2359328 | tf_op jit(solution)/shard_map/all_to_all | solution.py:122
  82.3 1.4 copy-done
  83.7 3.3 %copy.67 = f32[48,4,4,768]{3,2,0,1:T(4,128)S(1)} copy(f32[48,4,4,768]{3,0,2,1:T(8,128)} %bitcast.91) | data formatting | bytes 4718592 | tf_op jit(solution)/shard_map/all_to_all | solution.py:122
  87.1 1.5 bitcast_reduce_fusion
  88.6 1.8 copy.38
  90.5 3.8 %all_to_all.31 = f32[192,4,6,128]{3,2,0,1:T(8,128)} reshape(f32[4,48,4,768]{3,1,0,2:T(8,128)} %copy.38) | data formatting | bytes 4718592 | tf_op jit(solution)/shard_map/all_to_all | solution.py:122
  94.2 2.1 broadcast_subtract_fusion
  96.4 4.3 %fusion.51 = f32[4,6,32,192]{3,2,1,0:T(8,128)S(1)} fusion(f32[192,4,6,128]{3,2,0,1:T(8,128)S(1)} %broadcast_subtract_fusion, f32[4,6,32,128]{3,2,1,0:T(8,128)S(1)} %copy-done.4, f32[4,6]{1,0:T(4,128)S(1)} %convert_element_type.10), kind=kOutput, calls=%fused_computation.77 | convolution fusion | flops 226590720 | bytes 3342432 | tf_op jit(solution)/shard_map/rboc,mrbc->rbom/dot_general | solution.py:128
  101.7 2.1 convolution_bitcast_fusion.1
  105.0 44.0 %psum.15 = f32[192]{0:T(256)S(1)} all-reduce(f32[192]{0:T(256)S(1)} %bitcast.104), channel_id=1, replica_groups=mesh['group'=4,'dev'=8] {'group','dev'}, use_global_device_ids=true, to_apply=%region_7.8 | all-reduce | flops 192 | bytes 1536 | tf_op jit(solution)/shard_map/psum | solution.py:149
  149.0 83.6 %all-reduce.8.cloned.1.call-done = f32[192,192]{1,0:T(8,128)} async-done(((f32[192,192]{1,0:T(8,128)}), f32[192,192]{1,0:T(8,128)}) %all-reduce.8.cloned.1.call-update) | async-done | bytes 147472 | tf_op jit(solution)/shard_map/psum | solution.py:149
  232.6 1.6 abs_reduce_fusion
  234.2 1.6 fusion.62
  235.9 15.9 %while.13 = (s32[]{:T(128)}, f32[192,192]{0,1:T(8,128)S(1)}, f32[192,192]{1,0:T(8,128)S(1)}, s32[]{:T(128)}) while((s32[]{:T(128)}, f32[192,192]{0,1:T(8,128)S(1)}, f32[192,192]{1,0:T(8,128)S(1)}, s32[]{:T(128)}) %tuple.40), condition=%wide.region_6.7_spmd.clone, body=%wide.region_5.6_spmd.clone.sunk | while | flops 254951424 | bytes 1916981 | solution.py:77
  253.7 2.3 fusion.33
  256.0 1.5 copy.45
  257.6 30.3 %all_to_all.39 = f32[192,4,768]{2,1,0:T(4,128)S(1)} all-to-all(f32[192,4,768]{2,1,0:T(4,128)S(1)} %copy.45), channel_id=1, replica_groups=mesh['group'=4,'dev'=8] {'group'}, dimensions={0} | all-to-all | bytes 4718592 | tf_op jit(solution)/shard_map/all_to_all | solution.py:158
  288.5 1.9 all_to_all.36
  (134 shorter events, 29.3 us)
Async XLA Ops:
  8.1 19.2 %collective-permute-start.4 = (f32[1,3,768]{2,1,0:T(4,128)}, f32[1,3,768]{2,1,0:T(4,128)S(1)}, u32[]{:S(2)}, u32[]{:S(2)}) collective-permute-start(f32[1,3,768]{2,1,0:T(4,128)} %get-tuple-element.76), channel_id=1, source_target_pairs={{0,1},{1,2},{2,3},{3,4},{4,5},{5,6},{6,7},{8,9},{9,10},{10,11},{11... | collective-permute-start | bytes 27656 | tf_op jit(solution)/shard_map/ppermute | solution.py:26
  10.5 18.1 %collective-permute-start.5 = (f32[1,3,768]{2,1,0:T(4,128)}, f32[1,3,768]{2,1,0:T(4,128)S(1)}, u32[]{:S(2)}, u32[]{:S(2)}) collective-permute-start(f32[1,3,768]{2,1,0:T(4,128)} %get-tuple-element.77), channel_id=1, source_target_pairs={{1,0},{2,1},{3,2},{4,3},{5,4},{6,5},{7,6},{9,8},{10,9},{11,10},{12... | collective-permute-start | bytes 27656 | tf_op jit(solution)/shard_map/ppermute | solution.py:28
  12.4 18.2 %collective-permute-start.2 = (f32[1,3,768]{2,1,0:T(4,128)}, f32[1,3,768]{2,1,0:T(4,128)S(1)}, u32[]{:S(2)}, u32[]{:S(2)}) collective-permute-start(f32[1,3,768]{2,1,0:T(4,128)} %get-tuple-element.78), channel_id=1, source_target_pairs={{0,1},{1,2},{2,3},{3,4},{4,5},{5,6},{6,7},{8,9},{9,10},{10,11},{11... | collective-permute-start | bytes 27656 | tf_op jit(solution)/shard_map/ppermute | solution.py:26
  17.6 13.0 %collective-permute-start.3 = (f32[1,3,768]{2,1,0:T(4,128)S(1)}, f32[1,3,768]{2,1,0:T(4,128)S(1)}, u32[]{:S(2)}, u32[]{:S(2)}) collective-permute-start(f32[1,3,768]{2,1,0:T(4,128)S(1)} %get-tuple-element.79), channel_id=1, source_target_pairs={{1,0},{2,1},{3,2},{4,3},{5,4},{6,5},{7,6},{9,8},{10,9},{11,10},{12... | collective-permute-start | bytes 27656 | tf_op jit(solution)/shard_map/ppermute | solution.py:28
  20.7 10.6 %copy-start.3 = (f32[48,16,768]{2,1,0:T(8,128)S(1)}, f32[48,16,768]{2,1,0:T(8,128)}, u32[]{:S(2)}) copy-start(f32[48,16,768]{2,1,0:T(8,128)} %param.9) | copy-start | bytes 7077892
  21.6 9.7 %collective-permute-start = (f32[48,3,768]{2,0,1:T(8,128)}, f32[48,3,768]{2,0,1:T(8,128)S(1)}, u32[]{:S(2)}, u32[]{:S(2)}) collective-permute-start(f32[48,3,768]{2,0,1:T(8,128)} %copy.64), channel_id=1, source_target_pairs={{0,1},{1,2},{2,3},{3,4},{4,5},{5,6},{6,7},{8,9},{9,10},{10,11},{11... | collective-permute-start | bytes 1327112 | tf_op jit(solution)/shard_map/ppermute | solution.py:26
  27.3 5.4 %collective-permute-start.1 = (f32[48,3,768]{2,0,1:T(8,128)S(1)}, f32[48,3,768]{2,0,1:T(8,128)S(1)}, u32[]{:S(2)}, u32[]{:S(2)}) collective-permute-start(f32[48,3,768]{2,0,1:T(8,128)S(1)} %copy.65), channel_id=1, source_target_pairs={{1,0},{2,1},{3,2},{4,3},{5,4},{6,5},{7,6},{9,8},{10,9},{11,10},{12... | collective-permute-start | bytes 1327112 | tf_op jit(solution)/shard_map/ppermute | solution.py:28
  33.7 1.6 copy-start.6
  33.7 1.6 copy-start.7
  33.7 1.6 copy-start.12
  40.4 1.8 copy-start.2
  40.4 1.8 copy-start.5
  40.4 1.8 copy-start.11
  45.4 1.3 copy-start.8
  50.4 4.0 %copy-start.10 = (s32[4,6]{1,0:T(4,128)S(1)}, s32[4,6]{1,0:T(4,128)}, u32[]{:S(2)}) copy-start(s32[4,6]{1,0:T(4,128)} %param.14) | copy-start | bytes 292
  50.4 31.9 %all-to-all-start = ((f32[48,16,768]{2,0,1:T(8,128)}), f32[48,16,768]{2,0,1:T(8,128)S(1)}, u32[]{:S(2)}, u32[]{:S(2)}) async-start(f32[48,16,768]{2,0,1:T(8,128)} %fusion.39), calls=%async_computation | async-start | bytes 4718592 | tf_op jit(solution)/shard_map/all_to_all | solution.py:122
  54.3 178.3 %all-reduce.8.cloned.1.call-start = ((), (), s32[]{:S(2)}) async-start(), calls=%async_computation.2 | async-start | bytes 393216 | tf_op jit(solution)/shard_map/psum | solution.py:149
  82.3 1.4 copy-start
  83.7 3.3 %copy-start.1 = (f32[48,16,768]{2,0,1:T(8,128)S(1)}, f32[48,16,768]{2,0,1:T(8,128)}, u32[]{:S(2)}) copy-start(f32[48,16,768]{2,0,1:T(8,128)} %copy-done) | copy-start | bytes 7077892
  94.2 2.2 copy-start.4
  96.4 5.1 %copy-start.9 = (f32[4,6,32]{2,0,1:T(4,128)S(1)}, f32[4,6,32]{2,0,1:T(4,128)}, u32[]{:S(2)}) copy-start(f32[4,6,32]{2,0,1:T(4,128)} %param.15) | copy-start | bytes 9220
Sparse Core Ops, SparseCore 0:
  104.0 128.5 all-reduce.7
where the time goes:
time: 298 us; the launch traced here: 297 us
  waiting for transfers between devices  111 us (37%)
  blocking collectives  74.3 us (25%)
  other arithmetic  27.2 us (9%)
  matrix products  25.5 us (9%)
  local copies, waits for them, and re-layouts  23.9 us (8%)
  starting transfers between devices  19.9 us (7%)
  between operations  14.6 us (5%)
    psum x1, waiting for transfers between devices, body(): gram_total, rhs_total = lax.psum((gram_part, rhs_part), ('group', 'dev'))  83.6 us
    psum x1, blocking collectives, body(): gram_total, rhs_total = lax.psum((gram_part, rhs_part), ('group', 'dev'))  44 us
    all_to_all x1, blocking collectives, body(): lax.all_to_all(analysis, 'group', split_axis=0, concat_axis=1, tiled=True)  30.3 us
    all_to_all x1, waiting for transfers between devices, body(): lax.all_to_all(predict_heads, 'group', split_axis=1, concat_axis=0, tiled...  27.8 us
    ppermute x3, starting transfers between devices, padded(): lax.ppermute(tail, axis, [(i, (i + 1) % count) for i in range(ends)])  12 us
    mul x4, other arithmetic, soil_hydraulic_law(): hydraulic_conductance * factor  9.18 us
    all_to_all x3, local copies, waits for them, and re-layouts, body(): lax.all_to_all(predict_heads, 'group', split_axis=1, concat_axis=0, tiled...  8.92 us
    dot_general x12, matrix products, one_turn(): jnp.dot(iterate, middle, precision=highest, preferred_element_type=jnp.fl...  6.96 us
  transfers between devices with their start and end apart: 8, of which 2 were waited for; matrix products, arithmetic and copies ran while one was open for 3% of the time, Pallas kernels for 0%

commit v1 on v0

v1 whole, which is shorter than its diff:
```python
import functools

import jax
import jax.numpy as jnp
from jax import lax
from jax.experimental import pallas as pl
from jax.experimental.pallas import tpu as pltpu
from jax.sharding import PartitionSpec as P

MODEL_STEPS = 3
NEWTON_STEPS = 12
LANES = 128
SUBLANES = 8

step_duration = 0.1
gravity_head = 1.0
highest = lax.Precision.HIGHEST
MESH = pl.DeviceIdType.MESH
last_dims = (((1,), (1,)), ((), ()))


def soil_values(soil_index, ks_table, alpha_table):
    soil_kinds = jnp.arange(ks_table.shape[0], dtype=jnp.int32)
    one_hot = (soil_index[None] == soil_kinds[:, None, None]).astype(jnp.float32)
    return jnp.stack(
        [
            jnp.sum(one_hot * ks_table[:, None, None], axis=0),
            jnp.sum(one_hot * alpha_table[:, None, None], axis=0),
        ],
        axis=1,
    )


def place(group, dev):
    return {"group": group, "dev": dev}


def forecast_kernel(
    groups, devs, heads, soil, obs, fc, proj,
    ext_a, ext_b, soil_ext, obs_all,
    local_sem, obs_send, obs_recv, halo_send, halo_recv, soil_send, soil_recv,
):
    w = MODEL_STEPS
    rows, members, columns = heads.shape
    blocks = columns // LANES
    server_rows = rows // groups
    g = lax.axis_index("group")
    d = lax.axis_index("dev")
    first, last = d == 0, d == devs - 1

    own_heads = pltpu.make_async_copy(heads, ext_a.at[pl.ds(w, rows)], local_sem.at[0])
    own_soil = pltpu.make_async_copy(soil, soil_ext.at[pl.ds(w, rows)], local_sem.at[1])
    own_obs = pltpu.make_async_copy(obs, obs_all.at[g], local_sem.at[2])
    own_heads.start()
    own_soil.start()
    own_obs.start()

    barrier = pltpu.get_barrier_semaphore()
    for k in range(1, groups):
        pl.semaphore_signal(
            barrier, inc=1, device_id=place((g + k) % groups, d), device_id_type=MESH
        )

    @pl.when(d > 0)
    def _():
        pl.semaphore_signal(barrier, inc=1, device_id=place(g, d - 1), device_id_type=MESH)

    @pl.when(d < devs - 1)
    def _():
        pl.semaphore_signal(barrier, inc=1, device_id=place(g, d + 1), device_id_type=MESH)

    neighbours = (d > 0).astype(jnp.int32) + (d < devs - 1).astype(jnp.int32)
    pl.semaphore_wait(barrier, groups - 1 + neighbours)

    def halo(source, target, send, recv, side):
        start, put, to = ((0, w + rows, d - 1), (rows - w, 0, d + 1))[side]
        return pltpu.make_async_remote_copy(
            src_ref=source.at[pl.ds(start, w)],
            dst_ref=target.at[pl.ds(put, w)],
            send_sem=send.at[side],
            recv_sem=recv.at[side],
            device_id=place(g, to),
            device_id_type=MESH,
        )

    def halos(side):
        return (
            halo(soil, soil_ext, soil_send, soil_recv, side),
            halo(heads, ext_a, halo_send, halo_recv, side),
        )

    @pl.when(d > 0)
    def _():
        for c in halos(0):
            c.start()

    @pl.when(d < devs - 1)
    def _():
        for c in halos(1):
            c.start()

    def obs_copy(k):
        return pltpu.make_async_remote_copy(
            src_ref=obs,
            dst_ref=obs_all.at[g],
            send_sem=obs_send.at[k],
            recv_sem=obs_recv.at[k],
            device_id=place((g + k) % groups, d),
            device_id_type=MESH,
        )

    def obs_arrival(k):
        return pltpu.make_async_remote_copy(
            src_ref=obs,
            dst_ref=obs_all.at[(g + groups - k) % groups],
            send_sem=obs_send.at[k],
            recv_sem=obs_recv.at[k],
            device_id=place((g + k) % groups, d),
            device_id_type=MESH,
        )

    for k in range(1, groups):
        obs_copy(k).start()

    def advance(src, dst, out_shift, low, high):
        def chunk(c, carry):
            part = pl.ds(pl.multiple_of(c * SUBLANES, SUBLANES), SUBLANES)
            shape = (SUBLANES, columns)
            lane = lax.broadcasted_iota(jnp.int32, shape, 1)
            has_next = lane < columns - 1
            has_before = lane > 0

            def law(i):
                h = src[i, part, :]
                ks = jnp.broadcast_to(soil_ext[i, 0:1, :], shape)
                alpha = jnp.broadcast_to(soil_ext[i, 1:2, :], shape)
                factor = jnp.exp(alpha * jnp.minimum(h, 0.0))
                return h, ks * factor, 0.1 + 0.4 * alpha * factor

            def across(h, k, h_next, k_next):
                return 0.5 * (k + k_next) * (h_next - h)

            h0, k0, _ = law(low - 1)
            h1, k1, c1 = law(low)

            def row(i, state):
                h, k, cap, g_before = state
                h_next, k_next, cap_next = law(i + 1)
                g_now = across(h, k, h_next, k_next)
                h_right = pltpu.roll(h, columns - 1, 1)
                k_right = pltpu.roll(k, columns - 1, 1)
                f = 0.5 * (k + k_right) * (h_right - h - gravity_head)
                f = jnp.where(has_next, f, 0.0)
                f_left = pltpu.roll(f, 1, 1)
                inflow = (g_now - g_before) + (f - f_left)
                dst[i - out_shift, part, :] = h + step_duration * inflow / cap
                return h_next, k_next, cap_next, g_now

            lax.fori_loop(low, high, row, (h1, k1, c1, across(h0, k0, h1, k1)))
            return carry

        lax.fori_loop(0, members // SUBLANES, chunk, 0)

    def clear(ref, low, high):
        ref[low:high] = jnp.zeros((high - low,) + ref.shape[1:], jnp.float32)

    own_heads.wait()
    own_soil.wait()

    advance(ext_a, ext_b, 0, w + 1, w + rows - 1)

    @pl.when(d > 0)
    def _():
        for c in halos(0):
            c.wait_send()
        for c in halos(1):
            c.wait_recv()

    @pl.when(d < devs - 1)
    def _():
        for c in halos(1):
            c.wait_send()
        for c in halos(0):
            c.wait_recv()

    @pl.when(first)
    def _():
        clear(ext_a, 0, w)
        clear(soil_ext, 0, w)

    @pl.when(last)
    def _():
        clear(ext_a, w + rows, rows + 2 * w)
        clear(soil_ext, w + rows, rows + 2 * w)

    advance(ext_a, ext_b, 0, 1, w + 1)
    advance(ext_a, ext_b, 0, w + rows - 1, rows + 2 * w - 1)

    def outside(ref, low, high):
        @pl.when(first)
        def _():
            clear(ref, low, w)

        @pl.when(last)
        def _():
            clear(ref, w + rows, high)

    outside(ext_b, 1, rows + 2 * w - 1)
    advance(ext_b, ext_a, 0, 2, rows + 2 * w - 2)
    outside(ext_a, 2, rows + 2 * w - 2)
    advance(ext_a, fc, w, w, w + rows)

    own_obs.wait()
    for k in range(1, groups):
        obs_copy(k).wait_send()
        obs_arrival(k).wait_recv()

    width = obs_all.shape[1] // server_rows
    per_block = width // blocks
    pairs = 2
    halves = server_rows // pairs

    def project(t, carry):
        owner, half = t // halves, t % halves
        pieces = []
        for p in range(pairs):
            r = t * pairs + p
            for b in range(blocks):
                weights = obs_all[
                    owner,
                    pl.ds(
                        pl.multiple_of(((half * pairs + p) * blocks + b) * per_block, SUBLANES),
                        per_block,
                    ),
                    :,
                ]
                pieces.append(
                    lax.dot_general(
                        fc[r, :, b * LANES : (b + 1) * LANES],
                        weights,
                        last_dims,
                        precision=highest,
                        preferred_element_type=jnp.float32,
                    )
                )
        proj[owner, :, pl.ds(pl.multiple_of(half * pairs * width, LANES), pairs * width)] = (
            jnp.concatenate(pieces, axis=1)
        )
        return carry

    lax.fori_loop(0, rows // pairs, project, 0)


def analysis_kernel(
    groups, devs, proj, fc, values, res,
    proj_all, gath, part, recv_a, red, recv_b, tot, full, mix, send_buf,
    local_sem, proj_send, proj_recv, fc_send, fc_recv,
    a_send, a_recv, b_send, b_recv, c_send, c_recv, out_send, out_recv,
):
    g = lax.axis_index("group")
    d = lax.axis_index("dev")
    cores = 2
    levels = devs // cores
    z, core = d // cores, d % cores
    teams = groups * cores
    me = g * cores + core
    _, server_rows, share, columns = fc.shape
    members = groups * share
    chunk = members // teams

    own_fc = pltpu.make_async_copy(
        fc.at[g], gath.at[:, pl.ds(pl.multiple_of(g * share, SUBLANES), share), :], local_sem.at[0]
    )
    own_proj = pltpu.make_async_copy(proj.at[g], proj_all.at[g], local_sem.at[1])
    own_fc.start()
    own_proj.start()

    def team(k):
        q = (me + k) % teams
        return q, place(q // cores, z * cores + q % cores)

    barrier = pltpu.get_barrier_semaphore()
    for k in range(1, teams):
        pl.semaphore_signal(barrier, inc=1, device_id=team(k)[1], device_id_type=MESH)
    for k in range(1, levels):
        pl.semaphore_signal(
            barrier,
            inc=1,
            device_id=place(g, (z + k) % levels * cores + core),
            device_id_type=MESH,
        )
    pl.semaphore_wait(barrier, teams - 1 + levels - 1)

    def copy(src, dst, send, recv, to):
        return pltpu.make_async_remote_copy(
            src_ref=src, dst_ref=dst, send_sem=send, recv_sem=recv,
            device_id=to, device_id_type=MESH,
        )

    def peer(k):
        p = (g + k) % groups
        return p, place(p, d)

    def member_slot(p):
        return gath.at[:, pl.ds(pl.multiple_of(p * share, SUBLANES), share), :]

    def proj_copy(k, incoming):
        p, to = peer(k)
        slot = (g + groups - k) % groups if incoming else g
        return copy(proj.at[p], proj_all.at[slot], proj_send.at[k], proj_recv.at[k], to)

    def fc_copy(k, incoming):
        p, to = peer(k)
        slot = (g + groups - k) % groups if incoming else g
        return copy(fc.at[p], member_slot(slot), fc_send.at[k], fc_recv.at[k], to)

    for k in range(1, groups):
        proj_copy(k, False).start()
    for k in range(1, groups):
        fc_copy(k, False).start()
    own_proj.wait()
    for k in range(1, groups):
        proj_copy(k, True).wait_recv()

    observed = jnp.concatenate([proj_all[q] for q in range(groups)], axis=0)
    average = jnp.sum(observed, axis=0, keepdims=True) / members
    centred = observed - average
    innovation = values[...] - average
    extra = full.shape[2] - members
    padding = jnp.concatenate(
        [innovation, jnp.zeros((extra - 1, innovation.shape[1]), jnp.float32)], axis=0
    )
    gram_part = lax.dot_general(
        centred,
        jnp.concatenate([centred, padding], axis=0),
        last_dims,
        precision=highest,
        preferred_element_type=jnp.float32,
    )
    for q in range(teams):
        part[q] = gram_part[q * chunk : (q + 1) * chunk, :]

    def a_copy(k, incoming):
        q, to = team(k)
        slot = (me + teams - k) % teams if incoming else me
        return copy(part.at[q], recv_a.at[slot], a_send.at[k], a_recv.at[k], to)

    for k in range(1, teams):
        a_copy(k, False).start()
    total = part[me]
    for k in range(1, teams):
        a_copy(k, True).wait_recv()
        total = total + recv_a[(me + teams - k) % teams]
    red[...] = total
    recv_b[z] = total

    def b_copy(k, incoming):
        to = place(g, (z + k) % levels * cores + core)
        slot = (z + levels - k) % levels if incoming else z
        return copy(red, recv_b.at[slot], b_send.at[k], b_recv.at[k], to)

    for k in range(1, levels):
        b_copy(k, False).start()
    for k in range(1, levels):
        b_copy(k, True).wait_recv()
    total = recv_b[0]
    for q in range(1, levels):
        total = total + recv_b[q]
    tot[...] = total
    full[me] = total

    def c_copy(k, incoming):
        _, to = team(k)
        slot = (me + teams - k) % teams if incoming else me
        return copy(tot, full.at[slot], c_send.at[k], c_recv.at[k], to)

    for k in range(1, teams):
        c_copy(k, False).start()
    for k in range(1, teams):
        c_copy(k, True).wait_recv()

    summed = jnp.concatenate([full[q] for q in range(teams)], axis=0)
    square = (members, members)
    diagonal = lax.broadcasted_iota(jnp.int32, square, 0) == lax.broadcasted_iota(
        jnp.int32, square, 1
    )
    identity = jnp.where(diagonal, 1.0, 0.0).astype(jnp.float32)
    gram = summed[:, :members] + (members - 1.0) * identity
    rhs = summed[:, members : members + 1]
    norm_total = jnp.sum(jnp.abs(gram))

    def dot(a, b):
        return jnp.dot(a, b, precision=highest, preferred_element_type=jnp.float32)

    def turn(_, pair):
        iterate, inverse = pair
        middle = 0.5 * (3.0 * identity - dot(inverse, iterate))
        return dot(iterate, middle), dot(middle, inverse)

    _, inverse = lax.fori_loop(0, NEWTON_STEPS, turn, (gram / norm_total, identity))
    right = jnp.broadcast_to(rhs, (members, LANES))
    shift = dot(inverse, dot(inverse, right)) / norm_total
    mix[...] = (jnp.sqrt((members - 1.0) / norm_total) * inverse + shift[:, 0:1]).T

    own_fc.wait()
    for k in range(1, groups):
        fc_copy(k, True).wait_recv()

    def centre(s, carry):
        block = gath[s]
        gath[s] = block - jnp.sum(block, axis=0, keepdims=True) / members
        return carry

    lax.fori_loop(0, server_rows, centre, 0)

    def out_copy(k, s, incoming):
        p, to = peer(k)
        slot = (g + groups - k) % groups if incoming else g
        return copy(
            send_buf.at[k, s], res.at[slot, s], out_send.at[k, s], out_recv.at[k, s], to
        )

    def mixed(p, s):
        weights = mix[pl.ds(pl.multiple_of(p * share, SUBLANES), share), :]
        return dot(weights, gath[s])

    for k in range(1, groups):

        def send(s, carry):
            send_buf[k, s] = mixed(peer(k)[0], s)
            out_copy(k, s, False).start()
            return carry

        lax.fori_loop(0, server_rows, send, 0)

    def keep(s, carry):
        res[g, s] = mixed(g, s)
        return carry

    lax.fori_loop(0, server_rows, keep, 0)

    for k in range(1, groups):
        proj_copy(k, False).wait_send()
        fc_copy(k, False).wait_send()
    for k in range(1, teams):
        a_copy(k, False).wait_send()
        c_copy(k, False).wait_send()
    for k in range(1, levels):
        b_copy(k, False).wait_send()
    for k in range(1, groups):
        for s in range(server_rows):
            out_copy(k, s, False).wait_send()
            out_copy(k, s, True).wait_recv()


def body(groups, devs, heads, soil_index, ks_table, alpha_table, obs_op, obs_mask, obs_values):
    soil = soil_values(soil_index, ks_table, alpha_table)
    mask = obs_mask.astype(jnp.float32)
    weights = (obs_op * mask[:, :, None, None]).reshape(-1, obs_op.shape[-1])
    values = (obs_values * mask[:, :, None]).reshape(1, -1)
    share, rows, columns = heads.shape
    server_rows = rows // groups
    observations = weights.shape[0]
    members = groups * share
    vmem = pl.BlockSpec(memory_space=pltpu.VMEM)
    anywhere = pl.BlockSpec(memory_space=pl.ANY)
    dma = pltpu.SemaphoreType.DMA
    f32 = jnp.float32
    extended = rows + 2 * MODEL_STEPS

    fc, proj = pl.pallas_call(
        functools.partial(forecast_kernel, groups, devs),
        out_shape=(
            jax.ShapeDtypeStruct((rows, share, columns), f32),
            jax.ShapeDtypeStruct((groups, share, observations), f32),
        ),
        in_specs=[anywhere] * 3,
        out_specs=(vmem, vmem),
        scratch_shapes=[
            pltpu.VMEM((extended, share, columns), f32),
            pltpu.VMEM((extended, share, columns), f32),
            pltpu.VMEM((extended, 2, columns), f32),
            pltpu.VMEM((groups, observations, LANES), f32),
            dma((3,)),
            dma((groups,)),
            dma((groups,)),
            dma((2,)),
            dma((2,)),
            dma((2,)),
            dma((2,)),
        ],
        compiler_params=pltpu.CompilerParams(collective_id=0, has_side_effects=True),
        name="forecast",
    )(heads.transpose(1, 0, 2), soil, weights)

    cores = 2
    teams, levels = groups * cores, devs // cores
    chunk = members // teams
    wide = (members // LANES + 1) * LANES
    res = pl.pallas_call(
        functools.partial(analysis_kernel, groups, devs),
        out_shape=jax.ShapeDtypeStruct((groups, server_rows, share, columns), f32),
        in_specs=[anywhere, anywhere, vmem],
        out_specs=vmem,
        scratch_shapes=[
            pltpu.VMEM((groups, share, observations), f32),
            pltpu.VMEM((server_rows, members, columns), f32),
            pltpu.VMEM((teams, chunk, wide), f32),
            pltpu.VMEM((teams, chunk, wide), f32),
            pltpu.VMEM((chunk, wide), f32),
            pltpu.VMEM((levels, chunk, wide), f32),
            pltpu.VMEM((chunk, wide), f32),
            pltpu.VMEM((teams, chunk, wide), f32),
            pltpu.VMEM((members, members), f32),
            pltpu.VMEM((groups, server_rows, share, columns), f32),
            dma((2,)),
            dma((groups,)),
            dma((groups,)),
            dma((groups,)),
            dma((groups,)),
            dma((teams,)),
            dma((teams,)),
            dma((levels,)),
            dma((levels,)),
            dma((teams,)),
            dma((teams,)),
            dma((groups, server_rows)),
            dma((groups, server_rows)),
        ],
        compiler_params=pltpu.CompilerParams(collective_id=1, has_side_effects=True),
        name="analysis",
    )(proj, fc.reshape(groups, server_rows, share, columns), values)
    return res.reshape(rows, share, columns).transpose(1, 0, 2)


def solution(mesh):
    groups, devs = mesh.shape["group"], mesh.shape["dev"]
    placed = (
        P("group", "dev", None),
        P("dev", None),
        P(),
        P(),
        P(("dev", "group"), None, None, None),
        P(("dev", "group"), None),
        P(("dev", "group"), None, None),
    )
    return jax.shard_map(
        functools.partial(body, groups, devs),
        mesh=mesh,
        in_specs=placed,
        out_specs=P("group", "dev", None),
        check_vma=False,
    )
```

time: 298 us -> 164 us (0.55)
  Pallas kernels: 0 us -> 150 us
  waiting for transfers between devices: 111 us -> 0 us
  blocking collectives: 74.3 us -> 0 us
  matrix products: 25.5 us -> 0 us
  other arithmetic: 27.2 us -> 4.26 us
  starting transfers between devices: 19.9 us -> 0 us
  between operations: 14.6 us -> 0.05 us
  local copies, waits for them, and re-layouts: 23.9 us -> 9.72 us
    pallas_call x0 -> x2, Pallas kernels: none -> 150 us  [the longest x1 88.5 us: body(): pl.pallas_call(functools.partial(analysis_kernel, groups, devs), out_shap...]
    psum x1 -> x0, waiting for transfers between devices: 83.6 us -> none  [body(): gram_total, rhs_total = lax.psum((gram_part, rhs_part), ('group', 'dev'))]
    psum x1 -> x0, blocking collectives: 44 us -> none  [body(): gram_total, rhs_total = lax.psum((gram_part, rhs_part), ('group', 'dev'))]
    all_to_all x1 -> x0, blocking collectives: 30.3 us -> none  [body(): lax.all_to_all(analysis, 'group', split_axis=0, concat_axis=1, tiled=True)]
    all_to_all x1 -> x0, waiting for transfers between devices: 27.8 us -> none  [body(): lax.all_to_all(predict_heads, 'group', split_axis=1, concat_axis=0, tiled...]
    dot_general x43 -> x0, matrix products: 25.5 us -> none  [the longest x12 6.96 us: one_turn(): jnp.dot(iterate, middle, precision=highest, preferred_element_type=jnp.fl...]
    ppermute x6 -> x0, starting transfers between devices: 15.9 us -> none  [the longest x3 12 us: padded(): lax.ppermute(tail, axis, [(i, (i + 1) % count) for i in range(ends)])]
    mul x11 -> x2, other arithmetic: 13.5 us -> 1.91 us  [the longest x1 1.83 us: body(): weights = (obs_op * mask[:, :, None, None]).reshape(-1, obs_op.shape[-1])]
  transfers between devices with their start and end apart: 8 -> 0, of which waited for: 2 -> 0; matrix products, arithmetic and copies ran while one was open for 3% -> 0% of each run, Pallas kernels for 0% -> 0%
where the time goes in v1:
time: 164 us
  Pallas kernels  150 us (91%)
  local copies, waits for them, and re-layouts  9.72 us (6%)
  other arithmetic  4.26 us (3%)
    pallas_call x1, Pallas kernels, body(): pl.pallas_call(functools.partial(analysis_kernel, groups, devs), out_shap...  88.5 us
    pallas_call x1, Pallas kernels, body(): pl.pallas_call(functools.partial(forecast_kernel, groups, devs), out_shap...  61.4 us
    unnamed x3, local copies, waits for them, and re-layouts  4.44 us
    reshape x1, local copies, waits for them, and re-layouts, body(): return res.reshape(rows, share, columns).transpose(1, 0, 2)  4.44 us

profile of v1, /device:TPU:0, one launch (start us, length us, event | category | flops | bytes accessed | tf_op | source)
XLA Modules:
  0.0 163.9 jit_solution(13901811714059052763)
XLA Ops:
  0.0 0.9 select_reduce_fusion.1
  1.0 0.7 pad_maximum_fusion.soil
  1.8 0.7 convert_element_type.4
  2.4 1.8 %broadcast_multiply_fusion = f32[4,6,32,128]{3,2,1,0:T(8,128)} fusion(f32[4,6,32,128]{3,2,1,0:T(8,128)} %param.11, f32[4,6]{1,0:T(4,128)S(1)} %convert_element_type.4), kind=kLoop, calls=%fused_computation.5 | loop fusion | flops 98304 | bytes 786528 | tf_op jit(solution)/shard_map/mul | solution.py:459
  4.3 4.4 %copy.23 = f32[48,16,768]{2,0,1:T(8,128)} copy(f32[48,16,768]{2,1,0:T(8,128)} %param.7) | data formatting | bytes 4718592 | tf_op args[0]
  8.7 0.0 copy-start
  8.7 61.4 %forecast.1 = (f32[16,48,768]{2,1,0:T(8,128)}, f32[4,48,768]{2,1,0:T(8,128)}) custom-call(f32[16,48,768]{2,1,0:T(8,128)} %bitcast.9, f32[16,2,768]{2,1,0:T(2,128)} %pad_maximum_fusion.soil, f32[768,128]{1,0:T(8,128)} %bitcast.12), custom_call_target="tpu_custom_call" | custom-call | tf_op jit(solution)/shard_map/forecast/pallas_call | solution.py:471
  70.1 0.1 copy.17
  70.2 0.0 copy-done
  70.2 0.1 broadcast_multiply_fusion.1
  70.3 0.7 reshape.19.values
  70.9 88.5 %analysis.1 = f32[4,4,48,768]{3,2,1,0:T(8,128)} custom-call(f32[4,48,768]{2,1,0:T(8,128)} %get-tuple-element.7.proj, f32[4,4,48,768]{3,2,1,0:T(8,128)} %bitcast.11, f32[1,768]{1,0:T(1,128)} %reshape.19.values), custom_call_target="tpu_custom_call" | custom-call | tf_op jit(solution)/shard_map/analysis/pallas_call | solution.py:500
  159.4 4.4 %copy.22 = f32[16,48,768]{2,0,1:T(8,128)} copy(f32[16,48,768]{2,1,0:T(8,128)} %bitcast.10) | data formatting | bytes 4718592 | tf_op jit(solution)/shard_map/reshape | solution.py:533
  (3 shorter events, 0.1 us)
Async XLA Ops:
  8.7 61.5 %copy-start = (f32[4,6,32]{2,0,1:T(4,128)S(1)}, f32[4,6,32]{2,0,1:T(4,128)}, u32[]{:S(2)}) copy-start(f32[4,6,32]{2,0,1:T(4,128)} %param.13) | copy-start | bytes 9220

commit v2 on v1

--- a/solution.py
+++ b/solution.py
@@ -151,12 +151,13 @@
                 k_right = pltpu.roll(k, columns - 1, 1)
                 f = 0.5 * (k + k_right) * (h_right - h - gravity_head)
                 f = jnp.where(has_next, f, 0.0)
-                f_left = pltpu.roll(f, 1, 1)
+                f_left = 0.5 * (k + pltpu.roll(k, 1, 1)) * (h - pltpu.roll(h, 1, 1) - gravity_head)
+                f_left = jnp.where(has_before, f_left, 0.0)
                 inflow = (g_now - g_before) + (f - f_left)
                 dst[i - out_shift, part, :] = h + step_duration * inflow / cap
                 return h_next, k_next, cap_next, g_now
 
-            lax.fori_loop(low, high, row, (h1, k1, c1, across(h0, k0, h1, k1)))
+            lax.fori_loop(low, high, row, (h1, k1, c1, across(h0, k0, h1, k1)), unroll=2)
             return carry
 
         lax.fori_loop(0, members // SUBLANES, chunk, 0)
@@ -259,14 +260,9 @@
 ):
     g = lax.axis_index("group")
     d = lax.axis_index("dev")
-    cores = 2
-    levels = devs // cores
-    z, core = d // cores, d % cores
-    teams = groups * cores
-    me = g * cores + core
     _, server_rows, share, columns = fc.shape
     members = groups * share
-    chunk = members // teams
+    chunk = members // devs
 
     own_fc = pltpu.make_async_copy(
         fc.at[g], gath.at[:, pl.ds(pl.multiple_of(g * share, SUBLANES), share), :], local_sem.at[0]
@@ -275,21 +271,16 @@
     own_fc.start()
     own_proj.start()
 
-    def team(k):
-        q = (me + k) % teams
-        return q, place(q // cores, z * cores + q % cores)
-
     barrier = pltpu.get_barrier_semaphore()
-    for k in range(1, teams):
-        pl.semaphore_signal(barrier, inc=1, device_id=team(k)[1], device_id_type=MESH)
-    for k in range(1, levels):
+    for k in range(1, groups):
         pl.semaphore_signal(
-            barrier,
-            inc=1,
-            device_id=place(g, (z + k) % levels * cores + core),
-            device_id_type=MESH,
-        )
-    pl.semaphore_wait(barrier, teams - 1 + levels - 1)
+            barrier, inc=1, device_id=place((g + k) % groups, d), device_id_type=MESH
+        )
+    for k in range(1, devs):
+        pl.semaphore_signal(
+            barrier, inc=1, device_id=place(g, (d + k) % devs), device_id_type=MESH
+        )
+    pl.semaphore_wait(barrier, groups - 1 + devs - 1)
 
     def copy(src, dst, send, recv, to):
         return pltpu.make_async_remote_copy(
@@ -301,23 +292,23 @@
         p = (g + k) % groups
         return p, place(p, d)
 
-    def member_slot(p):
-        return gath.at[:, pl.ds(pl.multiple_of(p * share, SUBLANES), share), :]
+    def member_slot(p, s):
+        return gath.at[s, pl.ds(pl.multiple_of(p * share, SUBLANES), share), :]
 
     def proj_copy(k, incoming):
         p, to = peer(k)
         slot = (g + groups - k) % groups if incoming else g
         return copy(proj.at[p], proj_all.at[slot], proj_send.at[k], proj_recv.at[k], to)
 
-    def fc_copy(k, incoming):
+    def fc_copy(k, s, incoming):
         p, to = peer(k)
         slot = (g + groups - k) % groups if incoming else g
-        return copy(fc.at[p], member_slot(slot), fc_send.at[k], fc_recv.at[k], to)
+        return copy(fc.at[p, s], member_slot(slot, s), fc_send.at[k, s], fc_recv.at[k, s], to)
 
     for k in range(1, groups):
         proj_copy(k, False).start()
     for k in range(1, groups):
-        fc_copy(k, False).start()
+        fc_copy(k, 0, False).start()
     own_proj.wait()
     for k in range(1, groups):
         proj_copy(k, True).wait_recv()
@@ -337,49 +328,56 @@
         precision=highest,
         preferred_element_type=jnp.float32,
     )
-    for q in range(teams):
+    for q in range(devs):
         part[q] = gram_part[q * chunk : (q + 1) * chunk, :]
 
+    def slab(k):
+        q = (d + k) % devs
+        return q, place(g, q)
+
     def a_copy(k, incoming):
-        q, to = team(k)
-        slot = (me + teams - k) % teams if incoming else me
+        q, to = slab(k)
+        slot = (d + devs - k) % devs if incoming else d
         return copy(part.at[q], recv_a.at[slot], a_send.at[k], a_recv.at[k], to)
 
-    for k in range(1, teams):
+    for k in range(1, devs):
         a_copy(k, False).start()
-    total = part[me]
-    for k in range(1, teams):
+    total = part[d]
+    for k in range(1, devs):
         a_copy(k, True).wait_recv()
-        total = total + recv_a[(me + teams - k) % teams]
+        total = total + recv_a[(d + devs - k) % devs]
     red[...] = total
-    recv_b[z] = total
+    recv_b[g] = total
 
     def b_copy(k, incoming):
-        to = place(g, (z + k) % levels * cores + core)
-        slot = (z + levels - k) % levels if incoming else z
+        _, to = peer(k)
+        slot = (g + groups - k) % groups if incoming else g
         return copy(red, recv_b.at[slot], b_send.at[k], b_recv.at[k], to)
 
-    for k in range(1, levels):
+    for k in range(1, groups):
         b_copy(k, False).start()
-    for k in range(1, levels):
+    for s in range(1, server_rows):
+        for k in range(1, groups):
+            fc_copy(k, s, False).start()
+    for k in range(1, groups):
         b_copy(k, True).wait_recv()
     total = recv_b[0]
-    for q in range(1, levels):
+    for q in range(1, groups):
         total = total + recv_b[q]
     tot[...] = total
-    full[me] = total
+    full[d] = total
 
     def c_copy(k, incoming):
-        _, to = team(k)
-        slot = (me + teams - k) % teams if incoming else me
+        _, to = slab(k)
+        slot = (d + devs - k) % devs if incoming else d
         return copy(tot, full.at[slot], c_send.at[k], c_recv.at[k], to)
 
-    for k in range(1, teams):
+    for k in range(1, devs):
         c_copy(k, False).start()
-    for k in range(1, teams):
+    for k in range(1, devs):
         c_copy(k, True).wait_recv()
 
-    summed = jnp.concatenate([full[q] for q in range(teams)], axis=0)
+    summed = jnp.concatenate([full[q] for q in range(devs)], axis=0)
     square = (members, members)
     diagonal = lax.broadcasted_iota(jnp.int32, square, 0) == lax.broadcasted_iota(
         jnp.int32, square, 1
@@ -403,10 +401,10 @@
     mix[...] = (jnp.sqrt((members - 1.0) / norm_total) * inverse + shift[:, 0:1]).T
 
     own_fc.wait()
-    for k in range(1, groups):
-        fc_copy(k, True).wait_recv()
 
     def centre(s, carry):
+        for k in range(1, groups):
+            fc_copy(k, s, True).wait_recv()
         block = gath[s]
         gath[s] = block - jnp.sum(block, axis=0, keepdims=True) / members
         return carry
@@ -441,12 +439,12 @@
 
     for k in range(1, groups):
         proj_copy(k, False).wait_send()
-        fc_copy(k, False).wait_send()
-    for k in range(1, teams):
+        b_copy(k, False).wait_send()
+        for s in range(server_rows):
+            fc_copy(k, s, False).wait_send()
+    for k in range(1, devs):
         a_copy(k, False).wait_send()
         c_copy(k, False).wait_send()
-    for k in range(1, levels):
-        b_copy(k, False).wait_send()
     for k in range(1, groups):
         for s in range(server_rows):
             out_copy(k, s, False).wait_send()
@@ -493,9 +491,7 @@
         name="forecast",
     )(heads.transpose(1, 0, 2), soil, weights)
 
-    cores = 2
-    teams, levels = groups * cores, devs // cores
-    chunk = members // teams
+    chunk = members // devs
     wide = (members // LANES + 1) * LANES
     res = pl.pallas_call(
         functools.partial(analysis_kernel, groups, devs),
@@ -505,25 +501,25 @@
         scratch_shapes=[
             pltpu.VMEM((groups, share, observations), f32),
             pltpu.VMEM((server_rows, members, columns), f32),
-            pltpu.VMEM((teams, chunk, wide), f32),
-            pltpu.VMEM((teams, chunk, wide), f32),
+            pltpu.VMEM((devs, chunk, wide), f32),
+            pltpu.VMEM((devs, chunk, wide), f32),
             pltpu.VMEM((chunk, wide), f32),
-            pltpu.VMEM((levels, chunk, wide), f32),
+            pltpu.VMEM((groups, chunk, wide), f32),
             pltpu.VMEM((chunk, wide), f32),
-            pltpu.VMEM((teams, chunk, wide), f32),
+            pltpu.VMEM((devs, chunk, wide), f32),
             pltpu.VMEM((members, members), f32),
             pltpu.VMEM((groups, server_rows, share, columns), f32),
             dma((2,)),
             dma((groups,)),
             dma((groups,)),
+            dma((groups, server_rows)),
+            dma((groups, server_rows)),
+            dma((devs,)),
+            dma((devs,)),
             dma((groups,)),
             dma((groups,)),
-            dma((teams,)),
-            dma((teams,)),
-            dma((levels,)),
-            dma((levels,)),
-            dma((teams,)),
-            dma((teams,)),
+            dma((devs,)),
+            dma((devs,)),
             dma((groups, server_rows)),
             dma((groups, server_rows)),
         ],

time: 164 us -> 118 us (0.72)
  Pallas kernels: 150 us -> 103 us
    pallas_call x1, Pallas kernels: 61.4 us -> 30.2 us  [body(): pl.pallas_call(functools.partial(forecast_kernel, groups, devs), out_shap...]
    pallas_call x1, Pallas kernels: 88.5 us -> 73 us  [body(): pl.pallas_call(functools.partial(analysis_kernel, groups, devs), out_shap...]
where the time goes in v2:
time: 118 us; the launch traced here: 117 us
  Pallas kernels  103 us (87%)
  local copies, waits for them, and re-layouts  9.72 us (8%)
  other arithmetic  4.26 us (4%)
    pallas_call x1, Pallas kernels, body(): pl.pallas_call(functools.partial(analysis_kernel, groups, devs), out_shap...  73 us
    pallas_call x1, Pallas kernels, body(): pl.pallas_call(functools.partial(forecast_kernel, groups, devs), out_shap...  30.2 us
    unnamed x3, local copies, waits for them, and re-layouts  4.44 us
    reshape x1, local copies, waits for them, and re-layouts, body(): return res.reshape(rows, share, columns).transpose(1, 0, 2)  4.44 us

profile of v2, /device:TPU:0, one launch (start us, length us, event | category | flops | bytes accessed | tf_op | source)
XLA Modules:
  0.0 117.2 jit_solution(17224346407165989842)
XLA Ops:
  0.0 0.9 select_reduce_fusion.1
  1.0 0.7 pad_maximum_fusion.soil
  1.8 0.7 convert_element_type.4
  2.4 1.8 %broadcast_multiply_fusion = f32[4,6,32,128]{3,2,1,0:T(8,128)} fusion(f32[4,6,32,128]{3,2,1,0:T(8,128)} %param.11, f32[4,6]{1,0:T(4,128)S(1)} %convert_element_type.4), kind=kLoop, calls=%fused_computation.5 | loop fusion | flops 98304 | bytes 786528 | tf_op jit(solution)/shard_map/mul | solution.py:457
  4.3 4.4 %copy.23 = f32[48,16,768]{2,0,1:T(8,128)} copy(f32[48,16,768]{2,1,0:T(8,128)} %param.7) | data formatting | bytes 4718592 | tf_op args[0]
  8.7 0.0 copy-start
  8.7 30.2 %forecast.1 = (f32[16,48,768]{2,1,0:T(8,128)}, f32[4,48,768]{2,1,0:T(8,128)}) custom-call(f32[16,48,768]{2,1,0:T(8,128)} %bitcast.9, f32[16,2,768]{2,1,0:T(2,128)} %pad_maximum_fusion.soil, f32[768,128]{1,0:T(8,128)} %bitcast.12), custom_call_target="tpu_custom_call" | custom-call | tf_op jit(solution)/shard_map/forecast/pallas_call | solution.py:469
  38.9 0.1 copy.17
  39.0 0.0 copy-done
  39.0 0.1 broadcast_multiply_fusion.1
  39.1 0.7 reshape.19.values
  39.7 73.0 %analysis.1 = f32[4,4,48,768]{3,2,1,0:T(8,128)} custom-call(f32[4,48,768]{2,1,0:T(8,128)} %get-tuple-element.7.proj, f32[4,4,48,768]{3,2,1,0:T(8,128)} %bitcast.11, f32[1,768]{1,0:T(1,128)} %reshape.19.values), custom_call_target="tpu_custom_call" | custom-call | tf_op jit(solution)/shard_map/analysis/pallas_call | solution.py:496
  112.8 4.4 %copy.22 = f32[16,48,768]{2,0,1:T(8,128)} copy(f32[16,48,768]{2,1,0:T(8,128)} %bitcast.10) | data formatting | bytes 4718592 | tf_op jit(solution)/shard_map/reshape | solution.py:529
  (3 shorter events, 0.1 us)
Async XLA Ops:
  8.7 30.3 %copy-start = (f32[4,6,32]{2,0,1:T(4,128)S(1)}, f32[4,6,32]{2,0,1:T(4,128)}, u32[]{:S(2)}) copy-start(f32[4,6,32]{2,0,1:T(4,128)} %param.13) | copy-start | bytes 9220

commit v3 on v2

--- a/solution.py
+++ b/solution.py
@@ -38,20 +38,24 @@
 def forecast_kernel(
     groups, devs, heads, soil, obs, fc, proj,
     ext_a, ext_b, soil_ext, obs_all,
-    local_sem, obs_send, obs_recv, halo_send, halo_recv, soil_send, soil_recv,
+    row_sem, local_sem, obs_send, obs_recv, halo_send, halo_recv, soil_send, soil_recv,
 ):
     w = MODEL_STEPS
-    rows, members, columns = heads.shape
+    members, rows, columns = heads.shape
     blocks = columns // LANES
     server_rows = rows // groups
     g = lax.axis_index("group")
     d = lax.axis_index("dev")
     first, last = d == 0, d == devs - 1
 
-    own_heads = pltpu.make_async_copy(heads, ext_a.at[pl.ds(w, rows)], local_sem.at[0])
+    own_rows = [
+        pltpu.make_async_copy(heads.at[:, r, :], ext_a.at[w + r], row_sem.at[r])
+        for r in range(rows)
+    ]
     own_soil = pltpu.make_async_copy(soil, soil_ext.at[pl.ds(w, rows)], local_sem.at[1])
     own_obs = pltpu.make_async_copy(obs, obs_all.at[g], local_sem.at[2])
-    own_heads.start()
+    for c in own_rows:
+        c.start()
     own_soil.start()
     own_obs.start()
 
@@ -72,8 +76,11 @@
     neighbours = (d > 0).astype(jnp.int32) + (d < devs - 1).astype(jnp.int32)
     pl.semaphore_wait(barrier, groups - 1 + neighbours)
 
-    def halo(source, target, send, recv, side):
-        start, put, to = ((0, w + rows, d - 1), (rows - w, 0, d + 1))[side]
+    for c in own_rows:
+        c.wait()
+
+    def halo(source, target, send, recv, side, base):
+        start, put, to = ((base, w + rows, d - 1), (base + rows - w, 0, d + 1))[side]
         return pltpu.make_async_remote_copy(
             src_ref=source.at[pl.ds(start, w)],
             dst_ref=target.at[pl.ds(put, w)],
@@ -85,8 +92,8 @@
 
     def halos(side):
         return (
-            halo(soil, soil_ext, soil_send, soil_recv, side),
-            halo(heads, ext_a, halo_send, halo_recv, side),
+            halo(soil, soil_ext, soil_send, soil_recv, side, 0),
+            halo(ext_a, ext_a, halo_send, halo_recv, side, w),
         )
 
     @pl.when(d > 0)
@@ -157,7 +164,7 @@
                 dst[i - out_shift, part, :] = h + step_duration * inflow / cap
                 return h_next, k_next, cap_next, g_now
 
-            lax.fori_loop(low, high, row, (h1, k1, c1, across(h0, k0, h1, k1)), unroll=2)
+            lax.fori_loop(low, high, row, (h1, k1, c1, across(h0, k0, h1, k1)), unroll=4)
             return carry
 
         lax.fori_loop(0, members // SUBLANES, chunk, 0)
@@ -165,7 +172,6 @@
     def clear(ref, low, high):
         ref[low:high] = jnp.zeros((high - low,) + ref.shape[1:], jnp.float32)
 
-    own_heads.wait()
     own_soil.wait()
 
     advance(ext_a, ext_b, 0, w + 1, w + rows - 1)
@@ -393,9 +399,15 @@
     def turn(_, pair):
         iterate, inverse = pair
         middle = 0.5 * (3.0 * identity - dot(inverse, iterate))
-        return dot(iterate, middle), dot(middle, inverse)
-
-    _, inverse = lax.fori_loop(0, NEWTON_STEPS, turn, (gram / norm_total, identity))
+        both = dot(jnp.concatenate([iterate, inverse], axis=0), middle)
+        return both[:members], both[members:]
+
+    scaled = gram / norm_total
+    middle = 0.5 * (3.0 * identity - scaled)
+    iterate, inverse = lax.fori_loop(
+        0, NEWTON_STEPS - 2, turn, (dot(scaled, middle), middle)
+    )
+    inverse = dot(0.5 * (3.0 * identity - dot(inverse, iterate)), inverse)
     right = jnp.broadcast_to(rhs, (members, LANES))
     shift = dot(inverse, dot(inverse, right)) / norm_total
     mix[...] = (jnp.sqrt((members - 1.0) / norm_total) * inverse + shift[:, 0:1]).T
@@ -479,6 +491,7 @@
             pltpu.VMEM((extended, share, columns), f32),
             pltpu.VMEM((extended, 2, columns), f32),
             pltpu.VMEM((groups, observations, LANES), f32),
+            dma((rows,)),
             dma((3,)),
             dma((groups,)),
             dma((groups,)),
@@ -489,7 +502,7 @@
         ],
         compiler_params=pltpu.CompilerParams(collective_id=0, has_side_effects=True),
         name="forecast",
-    )(heads.transpose(1, 0, 2), soil, weights)
+    )(heads, soil, weights)
 
     chunk = members // devs
     wide = (members // LANES + 1) * LANES

time: 118 us -> 113 us (0.958)
  local copies, waits for them, and re-layouts: 9.72 us -> 5.28 us
    unnamed x3 -> x0, local copies, waits for them, and re-layouts: 4.44 us -> none
    pallas_call x1, Pallas kernels: 30.2 us -> 28.4 us  [body(): pl.pallas_call(functools.partial(forecast_kernel, groups, devs), out_shap...]
where the time goes in v3:
time: 113 us; the launch traced here: 112 us
  Pallas kernels  102 us (90%)
  local copies, waits for them, and re-layouts  5.28 us (5%)
  other arithmetic  4.96 us (4%)
    pallas_call x1, Pallas kernels, body(): pl.pallas_call(functools.partial(analysis_kernel, groups, devs), out_shap...  73.8 us
    pallas_call x1, Pallas kernels, body(): pl.pallas_call(functools.partial(forecast_kernel, groups, devs), out_shap...  28.4 us
    reshape x1, local copies, waits for them, and re-layouts, body(): return res.reshape(rows, share, columns).transpose(1, 0, 2)  4.44 us

profile of v3, /device:TPU:0, one launch (start us, length us, event | category | flops | bytes accessed | tf_op | source)
XLA Modules:
  0.0 112.5 jit_solution(4250905758906040739)
XLA Ops:
  0.0 0.7 convert_element_type.4
  0.7 0.1 copy.14
  0.8 0.8 broadcast_multiply_fusion.1
  1.6 0.7 reshape.19.values
  2.2 0.9 select_reduce_fusion.1
  3.3 0.7 pad_maximum_fusion.soil
  4.0 1.8 %broadcast_multiply_fusion = f32[4,6,32,128]{3,2,1,0:T(8,128)} fusion(f32[4,6,32,128]{3,2,1,0:T(8,128)} %param.11, f32[4,6]{1,0:T(4,128)S(1)} %convert_element_type.4), kind=kLoop, calls=%fused_computation.4 | loop fusion | flops 98304 | bytes 786528 | tf_op jit(solution)/shard_map/mul | solution.py:469
  5.8 28.4 %forecast.1 = (f32[16,48,768]{2,1,0:T(8,128)}, f32[4,48,768]{2,1,0:T(8,128)}) custom-call(f32[48,16,768]{2,1,0:T(8,128)} %heads.1, f32[16,2,768]{2,1,0:T(2,128)} %pad_maximum_fusion.soil, f32[768,128]{1,0:T(8,128)} %bitcast.8), custom_call_target="tpu_custom_call" | custom-call | tf_op jit(solution)/shard_map/forecast/pallas_call | solution.py:481
  34.3 73.8 %analysis.1 = f32[4,4,48,768]{3,2,1,0:T(8,128)} custom-call(f32[4,48,768]{2,1,0:T(8,128)} %get-tuple-element.7.proj, f32[4,4,48,768]{3,2,1,0:T(8,128)} %bitcast.7, f32[1,768]{1,0:T(1,128)} %reshape.19.values), custom_call_target="tpu_custom_call" | custom-call | tf_op jit(solution)/shard_map/analysis/pallas_call | solution.py:509
  108.1 4.4 %copy.18 = f32[16,48,768]{2,0,1:T(8,128)} copy(f32[16,48,768]{2,1,0:T(8,128)} %bitcast.6) | data formatting | bytes 4718592 | tf_op jit(solution)/shard_map/reshape | solution.py:542
  (3 shorter events, 0.1 us)
